TPU v7x, 32 devices: a whole 2x2x4 slice. The times are simulated.
32 devices in a mesh: scene: 4 (over x, core), view: 4 (over z), half: 2 (over y).
Axes of the slice: x: 2, y: 2, z: 4, core: 2. Of those that a mesh axis runs over, the one named last changes fastest.
Arguments:
- tokens: bfloat16 [16, 512, 2048], P(('scene', 'view'), 'half'), parts along dimension 0, may hold values from -9 to 12
- w_qkv: bfloat16 [2048, 768], replicated, may hold values from -0.125 to 0.125
- w_out: bfloat16 [256, 2048], replicated, may hold values from -5 to 5
- key_lists: int32 [16, 4, 2], P(('scene', 'view'), 'half'), parts along dimension 0, may hold values from 0 to 15, as said below
- list_len: int32 [16, 4], P(('scene', 'view'), 'half'), parts along dimension 0, may hold values from 1 to 2, as said below
Outputs:
- mixed: bfloat16 [16, 512, 2048], P(('scene', 'view'), 'half'), parts along dimension 0
There are 4 independent parts, one for each index of `scene`. A program takes and returns all parts, laid end to end along the dimension named above; an argument that names none is the same for every part. Nothing has to cross between parts.
Inputs may be any that keep to these rules, and one draw needn't show every extreme that they name: `key_lists`: entries of one list are distinct block ids of the scene. `list_len`: some query block lists 2 blocks in every scene.
All inputs are finite; a program needn't handle non-finite values.
Results may differ from a plain program's by a relative error of at most 0.014.
The roundings to bfloat16 on the way count: a program that leaves them out, or rounds other values in their place, can miss the bound.
Values may be sent and summed in bfloat16 or wider, within the bound.
A program may use at most 64 MiB of HBM per device.

v0:
```python
import functools

import jax
import jax.numpy as jnp
from jax import lax
from jax.experimental import pallas as pl
from jax.experimental.pallas import tpu as pltpu
from jax.sharding import PartitionSpec as P

HEADS = 4
NEG = -1e30
MESH = pl.DeviceIdType.MESH


def body(
    sizes,
    lists_ref,
    lens_ref,
    tokens_ref,
    w_ref,
    out_ref,
    x,
    w,
    kbuf,
    vbuf,
    weight_buf,
    total_buf,
    load_sem,
    send_sem,
    recv_sem,
):
    views, halves = sizes
    view, half = lax.axis_index("view"), lax.axis_index("half")
    count, block, inner = kbuf.shape
    local = count // (views * halves)
    rows = local * block
    head_size = inner // HEADS
    slots = lists_ref.shape[1]
    bufs = (kbuf, vbuf)

    loads = [pltpu.make_async_copy(tokens_ref, x, load_sem.at[0])]
    for n, group in enumerate((1, 2, 0)):
        cols = pl.ds(group * inner, inner)
        loads.append(
            pltpu.make_async_copy(w_ref.at[:, cols], w.at[group], load_sem.at[1 + n])
        )
    for load in loads[:2]:
        load.start()

    toward = (
        (view + 1 < views, {"view": view + 1}, views),
        (view >= 1, {"view": view - 1}, views),
        (half + 1 < halves, {"half": half + 1}, halves),
        (half >= 1, {"half": half - 1}, halves),
    )

    barrier = pltpu.get_barrier_semaphore()
    for there, device, size in toward:
        if size > 1:

            @pl.when(there)
            def _():
                pl.semaphore_signal(barrier, inc=1, device_id=device, device_id_type=MESH)

    def piece(c, slot, way):
        rows_of = bufs[c].at[slot]
        return pltpu.make_async_remote_copy(
            src_ref=rows_of,
            dst_ref=rows_of,
            send_sem=send_sem.at[way, c, slot],
            recv_sem=recv_sem.at[c, slot],
            device_id=toward[way][1],
            device_id_type=MESH,
        )

    sends = []

    def send(c, slot, way, here):
        there, _, size = toward[way]
        if size == 1:
            return
        cond = there if here is None else jnp.logical_and(here, there)
        sends.append((cond, c, slot, way))

        @pl.when(cond)
        def _():
            piece(c, slot, way).start()

    def arrive(c, slot, here):
        @pl.when(here)
        def _():
            piece(c, slot, 0).wait_recv()

    def project(group):
        return jnp.dot(x[...], w[group], preferred_element_type=jnp.float32).astype(
            jnp.bfloat16
        )

    own = view * halves + half
    loads[0].wait()
    for c in range(2):
        loads[1 + c].wait()
        loads[2 + c].start()
        for b in range(local):
            bufs[c][own * local + b] = jnp.dot(
                x[b * block : (b + 1) * block], w[1 + c], preferred_element_type=jnp.float32
            ).astype(jnp.bfloat16)
            if c == 0 and b == 0:
                expected = sum(there.astype(jnp.int32) for there, _, size in toward if size > 1)
                pl.semaphore_wait(barrier, expected)
            for way in (2, 3, 0, 1):
                send(c, own * local + b, way, None)

    loads[3].wait()
    queries = project(0)
    head_of = lax.broadcasted_iota(jnp.int32, (block, inner), 1) // head_size
    mine = [head_of == h for h in range(HEADS)]

    balanced = halves == 2 and views > 2
    last = views - 1

    def along_view(c, dist):
        for b in range(local):
            for sign, way in ((-1, 0), (1, 1)):
                shard = view + sign * dist
                here = shard >= 0 if sign < 0 else shard < views
                slot = (shard * halves + half) * local + b
                arrive(c, slot, here)
                across = here
                if balanced and c == 1:
                    across = shard >= 1 if sign < 0 else shard < last
                for out in (2, 3):
                    send(c, slot, out, across)
                if dist + 1 < views:
                    send(c, slot, way, here)

    def relay(dist):
        for b in range(local):
            for shard, here, way in ((0, view == dist, 0), (last, view == last - dist, 1)):
                slot = (shard * halves + (halves - 1) - half) * local + b
                arrive(1, slot, here)
                if dist < last:
                    send(1, slot, way, here)

    def along_half(c):
        for far in range(1, halves):
            for dist in range(views):
                for b in range(local):
                    for sign in (-1, 1) if dist else (1,):
                        shard = view + sign * dist
                        seen = shard >= 0 if sign < 0 else shard < views
                        if balanced and c == 1:
                            seen = jnp.logical_and(shard >= 1, shard < last)
                        for side, way in ((-1, 2), (1, 3)):
                            other = half + side * far
                            here = jnp.logical_and(
                                seen, other >= 0 if side < 0 else other < halves
                            )
                            slot = (shard * halves + other) * local + b
                            arrive(c, slot, here)
                            if far + 1 < halves:
                                send(c, slot, way, here)

    for dist in range(1, views):
        along_view(0, dist)
        if balanced and dist > 1:
            relay(dist - 1)
        along_view(1, dist)
        if balanced and dist == 1:
            relay(0)

    along_half(0)
    for i in range(local):
        q = queries[i * block : (i + 1) * block]
        stacked = jnp.concatenate([jnp.where(m, q, jnp.zeros_like(q)) for m in mine], axis=0)
        keys = jnp.concatenate([kbuf[lists_ref[i, s]] for s in range(slots)], axis=0)
        scores = lax.dot_general(
            stacked, keys, (((1,), (1,)), ((), ())), preferred_element_type=jnp.float32
        ) * head_size ** (-0.5)
        live = lax.broadcasted_iota(jnp.int32, scores.shape, 1) // block < lens_ref[i]
        top = jnp.max(jnp.where(live, scores, NEG), axis=1, keepdims=True)
        weights = jnp.where(live, jnp.exp(scores - top), 0.0)
        total_buf[i] = jnp.sum(weights, axis=1, keepdims=True)
        weight_buf[i] = weights.astype(jnp.bfloat16)

    along_half(1)
    if balanced:
        relay(last)
    for i in range(local):
        values = jnp.concatenate([vbuf[lists_ref[i, s]] for s in range(slots)], axis=0)
        summed = jnp.dot(weight_buf[i], values, preferred_element_type=jnp.float32)
        scaled = summed / total_buf[i]
        attn = jnp.zeros((block, inner), jnp.float32)
        for h, m in enumerate(mine):
            attn = jnp.where(m, scaled[h * block : (h + 1) * block], attn)
        out_ref[i * block : (i + 1) * block] = attn.astype(out_ref.dtype)

    for cond, c, slot, way in sends:

        @pl.when(cond)
        def _():
            piece(c, slot, way).wait_send()


def per_device(sizes, tokens, w_qkv, w_out, key_lists, list_len):
    views, halves = sizes
    rows, width = tokens.shape[1:]
    inner = w_out.shape[0]
    local = key_lists.shape[1]
    slots = key_lists.shape[2]
    block = rows // local
    shards = views * halves
    anywhere = pl.BlockSpec(memory_space=pl.ANY)
    attn = pl.pallas_call(
        functools.partial(body, sizes),
        out_shape=jax.ShapeDtypeStruct((rows, inner), jnp.bfloat16),
        in_specs=[
            pl.BlockSpec(memory_space=pltpu.SMEM),
            pl.BlockSpec(memory_space=pltpu.SMEM),
            anywhere,
            anywhere,
        ],
        out_specs=pl.BlockSpec(memory_space=pltpu.VMEM),
        scratch_shapes=[
            pltpu.VMEM((rows, width), jnp.bfloat16),
            pltpu.VMEM((3, width, inner), jnp.bfloat16),
            pltpu.VMEM((shards * local, block, inner), jnp.bfloat16),
            pltpu.VMEM((shards * local, block, inner), jnp.bfloat16),
            pltpu.VMEM((local, HEADS * block, slots * block), jnp.bfloat16),
            pltpu.VMEM((local, HEADS * block, 1), jnp.float32),
            pltpu.SemaphoreType.DMA((4,)),
            pltpu.SemaphoreType.DMA((4, 2, shards * local)),
            pltpu.SemaphoreType.DMA((2, shards * local)),
        ],
        compiler_params=pltpu.CompilerParams(collective_id=0, has_side_effects=True),
    )(
        key_lists.reshape(local, slots),
        list_len.reshape(local),
        tokens.reshape(rows, width),
        w_qkv,
    )
    mixed = jnp.dot(attn, w_out, preferred_element_type=jnp.float32).astype(jnp.bfloat16)
    return mixed.reshape(1, rows, width)


def solution(mesh):
    sizes = (mesh.shape["view"], mesh.shape["half"])
    placed = (
        P(("scene", "view"), "half", None),
        P(),
        P(),
        P(("scene", "view"), "half", None),
        P(("scene", "view"), "half"),
    )
    return jax.shard_map(
        functools.partial(per_device, sizes),
        mesh=mesh,
        in_specs=placed,
        out_specs=P(("scene", "view"), "half", None),
        check_vma=False,
    )
```

profile of v0, /device:TPU:0, one launch (start us, length us, event | category | flops | bytes accessed | tf_op | source)
XLA Modules:
  0.0 31.9 jit_solution(5003831197618841135)
XLA Ops:
  0.0 0.0 copy-start
  0.0 29.5 %shard_map.55 = bf16[256,256]{1,0:T(8,128)(2,1)} custom-call(s32[2,2]{1,0:T(2,128)} %bitcast.8, s32[2]{0:T(128)} %bitcast.9, bf16[256,2048]{1,0:T(8,128)(2,1)} %bitcast.7, bf16[2048,768]{1,0:T(8,128)(2,1)} %w_ref.1), custom_call_target="tpu_custom_call" | custom-call | tf_op jit(solution)/shard_map/pallas_call | solution.py:214
  29.6 0.0 copy-done
  29.6 2.3 %fusion = bf16[1,256,2048]{2,1,0:T(8,128)(2,1)} fusion(bf16[256,256]{1,0:T(8,128)(2,1)} %shard_map.55, bf16[256,2048]{1,0:T(8,128)(2,1)S(1)} %copy-done), kind=kOutput, calls=%fused_computation.1 | convolution fusion | flops 268959744 | bytes 2228224 | tf_op jit(solution)/shard_map/dot_general | solution.py:242
Async XLA Ops:
  0.0 29.6 %copy-start = (bf16[256,2048]{1,0:T(8,128)(2,1)S(1)}, bf16[256,2048]{1,0:T(8,128)(2,1)}, u32[]{:S(2)}) copy-start(bf16[256,2048]{1,0:T(8,128)(2,1)} %param.7) | copy-start | bytes 3145732
where the time goes:
time: 32.1 us; the launch traced here: 31.9 us
  Pallas kernels  29.5 us (92%)
  matrix products  2.32 us (7%)
    pallas_call x1, Pallas kernels, per_device(): pl.pallas_call(functools.partial(body, sizes), out_shape=jax.ShapeDtypeSt...  29.5 us
    dot_general x1, matrix products, per_device(): jnp.dot(attn, w_out, preferred_element_type=jnp.float32)  2.32 us

commit v1 on v0

--- a/solution.py
+++ b/solution.py
@@ -14,8 +14,8 @@
 
 def body(
     sizes,
-    lists_ref,
-    lens_ref,
+    lists_hbm,
+    lens_hbm,
     tokens_ref,
     w_ref,
     out_ref,
@@ -28,6 +28,10 @@
     load_sem,
     send_sem,
     recv_sem,
+    lists_ref,
+    lens_ref,
+    small_sem,
+    xsem,
 ):
     views, halves = sizes
     view, half = lax.axis_index("view"), lax.axis_index("half")
@@ -36,16 +40,24 @@
     rows = local * block
     head_size = inner // HEADS
     slots = lists_ref.shape[1]
+    small = [pltpu.make_async_copy(lists_hbm, lists_ref, small_sem.at[0]), pltpu.make_async_copy(lens_hbm, lens_ref, small_sem.at[1])]
     bufs = (kbuf, vbuf)
 
-    loads = [pltpu.make_async_copy(tokens_ref, x, load_sem.at[0])]
+    loads = []
     for n, group in enumerate((1, 2, 0)):
         cols = pl.ds(group * inner, inner)
         loads.append(
-            pltpu.make_async_copy(w_ref.at[:, cols], w.at[group], load_sem.at[1 + n])
+            pltpu.make_async_copy(w_ref.at[:, cols], w.at[group], load_sem.at[n])
         )
-    for load in loads[:2]:
-        load.start()
+    xl = [pltpu.make_async_copy(tokens_ref.at[pl.ds(b * block, block)], x.at[pl.ds(b * block, block)], xsem.at[b]) for b in range(local)]
+    xl[0].start()
+    loads[0].start()
+    for l in xl[1:]:
+        l.start()
+    for l in loads[1:]:
+        l.start()
+    for cp in small:
+        cp.start()
 
     toward = (
         (view + 1 < views, {"view": view + 1}, views),
@@ -97,11 +109,11 @@
         )
 
     own = view * halves + half
-    loads[0].wait()
     for c in range(2):
-        loads[1 + c].wait()
-        loads[2 + c].start()
+        loads[c].wait()
         for b in range(local):
+            if c == 0:
+                xl[b].wait()
             bufs[c][own * local + b] = jnp.dot(
                 x[b * block : (b + 1) * block], w[1 + c], preferred_element_type=jnp.float32
             ).astype(jnp.bfloat16)
@@ -111,7 +123,9 @@
             for way in (2, 3, 0, 1):
                 send(c, own * local + b, way, None)
 
-    loads[3].wait()
+    loads[2].wait()
+    for cp in small:
+        cp.wait()
     queries = project(0)
     head_of = lax.broadcasted_iota(jnp.int32, (block, inner), 1) // head_size
     mine = [head_of == h for h in range(HEADS)]
@@ -210,13 +224,13 @@
     slots = key_lists.shape[2]
     block = rows // local
     shards = views * halves
-    anywhere = pl.BlockSpec(memory_space=pl.ANY)
+    anywhere = pl.BlockSpec(memory_space=pltpu.HBM)
     attn = pl.pallas_call(
         functools.partial(body, sizes),
-        out_shape=jax.ShapeDtypeStruct((rows, inner), jnp.bfloat16),
+        out_shape=pltpu.VMEM((rows, inner), jnp.bfloat16),
         in_specs=[
-            pl.BlockSpec(memory_space=pltpu.SMEM),
-            pl.BlockSpec(memory_space=pltpu.SMEM),
+            anywhere,
+            anywhere,
             anywhere,
             anywhere,
         ],
@@ -231,8 +245,12 @@
             pltpu.SemaphoreType.DMA((4,)),
             pltpu.SemaphoreType.DMA((4, 2, shards * local)),
             pltpu.SemaphoreType.DMA((2, shards * local)),
+            pltpu.SMEM((local, slots), jnp.int32),
+            pltpu.SMEM((local,), jnp.int32),
+            pltpu.SemaphoreType.DMA((2,)),
+            pltpu.SemaphoreType.DMA((local,)),
         ],
-        compiler_params=pltpu.CompilerParams(collective_id=0, has_side_effects=True),
+        compiler_params=pltpu.CompilerParams(collective_id=0, has_side_effects=True, vmem_limit_bytes=62000000),
     )(
         key_lists.reshape(local, slots),
         list_len.reshape(local),

time: 32.1 us -> 29.6 us (0.922)
  Pallas kernels: 29.5 us -> 28 us
  matrix products: 2.32 us -> 1.42 us
    pallas_call x1, Pallas kernels: 29.5 us -> 28 us  [per_device(): pl.pallas_call(functools.partial(body, sizes), out_shape=pltpu.VMEM((rows...]
    dot_general x1, matrix products: 2.32 us -> 1.42 us  [per_device(): jnp.dot(attn, w_out, preferred_element_type=jnp.float32)]
where the time goes in v1:
time: 29.6 us; the launch traced here: 29.5 us
  Pallas kernels  28 us (95%)
  matrix products  1.42 us (5%)
    pallas_call x1, Pallas kernels, per_device(): pl.pallas_call(functools.partial(body, sizes), out_shape=pltpu.VMEM((rows...  28 us
    dot_general x1, matrix products, per_device(): jnp.dot(attn, w_out, preferred_element_type=jnp.float32)  1.42 us

profile of v1, /device:TPU:0, one launch (start us, length us, event | category | flops | bytes accessed | tf_op | source)
XLA Modules:
  0.0 29.5 jit_solution(3265437606536381830)
XLA Ops:
  0.0 0.0 copy-start
  0.0 28.0 %shard_map.55 = bf16[256,256]{1,0:T(8,128)(2,1)S(1)} custom-call(s32[2,2]{1,0:T(2,128)} %bitcast.8, s32[2]{0:T(128)} %bitcast.9, bf16[256,2048]{1,0:T(8,128)(2,1)} %bitcast.7, bf16[2048,768]{1,0:T(8,128)(2,1)} %w_ref.1), custom_call_target="tpu_custom_call" | custom-call | tf_op jit(solution)/shard_map/pallas_call | solution.py:228
  28.0 0.0 copy-done
  28.0 1.4 %fusion = bf16[1,256,2048]{2,1,0:T(8,128)(2,1)} fusion(bf16[256,256]{1,0:T(8,128)(2,1)S(1)} %shard_map.55, bf16[256,2048]{1,0:T(8,128)(2,1)S(1)} %copy-done), kind=kOutput, calls=%fused_computation.1 | convolution fusion | flops 268959744 | bytes 2228224 | tf_op jit(solution)/shard_map/dot_general | solution.py:260
Async XLA Ops:
  0.0 28.0 %copy-start = (bf16[256,2048]{1,0:T(8,128)(2,1)S(1)}, bf16[256,2048]{1,0:T(8,128)(2,1)}, u32[]{:S(2)}) copy-start(bf16[256,2048]{1,0:T(8,128)(2,1)} %param.7) | copy-start | bytes 3145732

commit v2 on v1

--- a/solution.py
+++ b/solution.py
@@ -216,6 +216,405 @@
             piece(c, slot, way).wait_send()
 
 
+def listed(entries, block):
+    hit = entries[0] == block
+    for entry in entries[1:]:
+        hit = jnp.logical_or(hit, entry == block)
+    return hit.astype(jnp.int32)
+
+
+def places(flags, count):
+    slots, after = [], 0
+    for flag in reversed(flags):
+        slots.append(jnp.where(flag == 1, count - 1 - after, -1))
+        after = after + flag
+    return slots[::-1]
+
+
+def chosen(slots, values, slot, empty):
+    out = empty
+    for s, value in zip(slots, values):
+        out = jnp.where(s == slot, value, out)
+    return out
+
+
+def paired_body(
+    sizes,
+    lists_hbm,
+    lens_hbm,
+    tokens_ref,
+    w_ref,
+    out_ref,
+    x,
+    w,
+    kbuf,
+    vbuf,
+    zstage,
+    ystage,
+    weight_buf,
+    total_buf,
+    x_sem,
+    w_sem,
+    small_sem,
+    send_sem,
+    recv_sem,
+    list_send_sem,
+    list_recv_sem,
+    *small,
+):
+    views, halves = sizes
+    view, half = lax.axis_index("view"), lax.axis_index("half")
+    block, inner = kbuf.shape[1:]
+    local = x.shape[0] // block
+    head_size = inner // HEADS
+    lists, lens = small[:4], small[4:]
+    slots = lists[0].shape[1]
+    bufs = (kbuf, vbuf)
+    quota = local * slots
+
+    loads = [
+        pltpu.make_async_copy(
+            tokens_ref.at[pl.ds(b * block, block)], x.at[pl.ds(b * block, block)], x_sem.at[b]
+        )
+        for b in range(local)
+    ]
+    w_loads = [
+        pltpu.make_async_copy(w_ref.at[:, pl.ds(group * inner, inner)], w.at[group], w_sem.at[n])
+        for n, group in enumerate((1, 2, 0))
+    ]
+    own_lists = [
+        pltpu.make_async_copy(lists_hbm, lists[0], small_sem.at[0]),
+        pltpu.make_async_copy(lens_hbm, lens[0], small_sem.at[1]),
+    ]
+    for load in (loads[0], w_loads[0], *loads[1:], *w_loads[1:], *own_lists):
+        load.start()
+
+    left = view < views // 2
+    end_view = jnp.where(left, 0, views - 1)
+    inner_view = jnp.where(left, 1, views - 2)
+    cross_view = views - 1 - inner_view
+    far_view = views - 1 - end_view
+    at_end = view == end_view
+    mate_view = jnp.where(at_end, inner_view, end_view)
+    other = halves - 1 - half
+    mate = {"view": mate_view}
+    beside = {"half": other}
+    diagonal = {"view": mate_view, "half": other}
+    cross = {"view": cross_view}
+
+    barrier = pltpu.get_barrier_semaphore()
+    for device in (mate, beside, diagonal):
+        pl.semaphore_signal(barrier, inc=1, device_id=device, device_id_type=MESH)
+
+    @pl.when(jnp.logical_not(at_end))
+    def _():
+        pl.semaphore_signal(barrier, inc=1, device_id=cross, device_id_type=MESH)
+
+    links = (mate, beside, cross)
+
+    def copy(c, link, n, src, to):
+        return pltpu.make_async_remote_copy(
+            src_ref=src,
+            dst_ref=bufs[c].at[to],
+            send_sem=send_sem.at[c, link, n],
+            recv_sem=recv_sem.at[c, to],
+            device_id=links[link],
+            device_id_type=MESH,
+        )
+
+    def arrived(c, *slots_of):
+        for to in slots_of:
+            copy(c, 0, 0, bufs[c].at[to], to).wait_recv()
+
+    def list_copies(to, device, n):
+        return [
+            pltpu.make_async_remote_copy(
+                src_ref=src,
+                dst_ref=dst,
+                send_sem=list_send_sem.at[n, k],
+                recv_sem=list_recv_sem.at[to, k],
+                device_id=device,
+                device_id_type=MESH,
+            )
+            for k, (src, dst) in enumerate(((lists_hbm, lists[to]), (lens_hbm, lens[to])))
+        ]
+
+    list_routes = ((1, beside), (2, mate), (3, diagonal))
+
+    def project(c, b):
+        bufs[c][b] = jnp.dot(
+            x[b * block : (b + 1) * block], w[1 + c], preferred_element_type=jnp.float32
+        ).astype(jnp.bfloat16)
+
+    last = local - 1
+    z_first, z_rest = local, local + 1
+    z_count = quota
+    over = 4 * local
+    picks_inner, picks_end = over + 1, z_rest + z_count
+
+    def own_sends(c, b):
+        @pl.when(at_end)
+        def _():
+            copy(c, 0, b, bufs[c].at[b], local + b).start()
+
+        @pl.when(jnp.logical_not(at_end))
+        def _():
+            copy(c, 2, b, bufs[c].at[b], 2 * local + b).start()
+            if b == 0:
+                copy(c, 0, 0, bufs[c].at[0], z_first).start()
+            if b == last:
+                copy(c, 1, 0, bufs[c].at[last], over).start()
+
+    for c in range(2):
+        w_loads[c].wait()
+        for b in range(local):
+            if c == 0:
+                loads[b].wait()
+            project(c, b)
+            if c == 0 and b == 0:
+                pl.semaphore_wait(barrier, jnp.where(at_end, 3, 4))
+                for n, (to, device) in enumerate(list_routes):
+                    for send in list_copies(to, device, n):
+                        send.start()
+            own_sends(c, b)
+
+    w_loads[2].wait()
+    queries = jnp.dot(x[...], w[0], preferred_element_type=jnp.float32).astype(jnp.bfloat16)
+    for load in own_lists:
+        load.wait()
+    for n, (to, device) in enumerate(list_routes):
+        for send in list_copies(to, device, n):
+            send.wait_recv()
+
+    def entries(k):
+        return [
+            jnp.where(s < lens[k][i], lists[k][i, s], -1) for i in range(local) for s in range(slots)
+        ]
+
+    def ids(of_view, of_half):
+        return [(of_view * halves + of_half) * local + b for b in range(local)]
+
+    mine, theirs = entries(0), entries(1)
+
+    def passed(ends):
+        inners, crosses, fars = (
+            [ids(v, h) for h in (half, other)] for v in (inner_view, cross_view, far_view)
+        )
+        needs, totals = [], []
+        for r in range(2):
+            needs.append([listed(ends, i) for i in (inners[r][last], *crosses[r], *fars[r])])
+            totals.append(sum(needs[r]))
+        out = []
+        for r in range(2):
+            spill = (totals[r] > z_count).astype(jnp.int32)
+            take = (totals[1 - r] > z_count).astype(jnp.int32)
+            flags = [needs[r][0] * (1 - spill), take, *needs[r][1:]]
+            names = [inners[r][last], inners[1 - r][last], *crosses[r], *fars[r]]
+            out.append((names, places(flags, z_count)))
+        return out
+
+    def positions(names, slots_of, first):
+        out = []
+        for entry in mine:
+            at = 0
+            for name, slot in zip(names, slots_of):
+                at = jnp.where(jnp.logical_and(entry == name, slot >= 0), first + slot, at)
+            out.append(at)
+        return out
+
+    def merge(*tables):
+        return [functools.reduce(jnp.maximum, column) for column in zip(*tables)]
+
+    def stage(c, stage_buf, k, slots_of, sources, count):
+        reach = k + len(sources) - count + 1
+        value = bufs[c][sources[0]]
+        for j in range(1, reach):
+            value = jnp.where(slots_of[j] == k, bufs[c][sources[j]], value)
+        stage_buf[c, k] = value
+
+    head_of = lax.broadcasted_iota(jnp.int32, (block, inner), 1) // head_size
+    heads = [head_of == h for h in range(HEADS)]
+
+    def weigh(at):
+        for i in range(local):
+            q = queries[i * block : (i + 1) * block]
+            stacked = jnp.concatenate([jnp.where(m, q, jnp.zeros_like(q)) for m in heads], axis=0)
+            keys = jnp.concatenate([kbuf[at[i * slots + s]] for s in range(slots)], axis=0)
+            scores = lax.dot_general(
+                stacked, keys, (((1,), (1,)), ((), ())), preferred_element_type=jnp.float32
+            ) * head_size ** (-0.5)
+            live = lax.broadcasted_iota(jnp.int32, scores.shape, 1) // block < lens[0][i]
+            top = jnp.max(jnp.where(live, scores, NEG), axis=1, keepdims=True)
+            weights = jnp.where(live, jnp.exp(scores - top), 0.0)
+            total_buf[i] = jnp.sum(weights, axis=1, keepdims=True)
+            weight_buf[i] = weights.astype(jnp.bfloat16)
+
+    def finish(at):
+        for i in range(local):
+            values = jnp.concatenate([vbuf[at[i * slots + s]] for s in range(slots)], axis=0)
+            summed = jnp.dot(weight_buf[i], values, preferred_element_type=jnp.float32)
+            scaled = summed / total_buf[i]
+            attn = jnp.zeros((block, inner), jnp.float32)
+            for h, m in enumerate(heads):
+                attn = jnp.where(m, scaled[h * block : (h + 1) * block], attn)
+            out_ref[i * block : (i + 1) * block] = attn.astype(out_ref.dtype)
+
+    def sent(c, link, n):
+        copy(c, link, n, bufs[c].at[0], 0).wait_send()
+
+    @pl.when(jnp.logical_not(at_end))
+    def _():
+        own, ends, crosses, fars = (
+            [g * local + b for b in range(local)] for g in range(4)
+        )
+        z_slots = passed(entries(2) + entries(3))[0][1]
+        z_sources = [own[last], over, *crosses, *fars]
+        groups = (inner_view, end_view, cross_view, far_view)
+
+        def order(table):
+            o, e, k, f = table
+            mixed = [v for pair in zip(e, k) for v in pair]
+            return [*o[:last], e[0], k[0], *mixed[2:], *f]
+
+        y_sources = order((own, ends, crosses, fars))
+
+        def picks(listing, of_half):
+            names = order([ids(v, of_half) for v in groups])
+            return names, places([listed(listing, name) for name in names], quota)
+
+        y_slots = picks(theirs, half)[1]
+        in_names, in_slots = picks(mine, other)
+        row = [i for v in groups for i in ids(v, half)]
+        at = merge(
+            positions(row, [jnp.int32(j) for j in range(len(row))], 0),
+            positions([ids(inner_view, other)[last]], [jnp.int32(0)], over),
+            positions(in_names, in_slots, picks_inner),
+        )
+
+        def z(c, k):
+            stage(c, zstage, k, z_slots, z_sources, z_count)
+            copy(c, 0, 1 + k, zstage.at[c, k], z_rest + k).start()
+
+        def y(c, k):
+            stage(c, ystage, k, y_slots, y_sources, quota)
+            copy(c, 1, 1 + k, ystage.at[c, k], picks_inner + k).start()
+
+        for c in range(2):
+            for b in range(local):
+                arrived(c, ends[b])
+                copy(c, 2, local + b, bufs[c].at[ends[b]], 3 * local + b).start()
+                arrived(c, crosses[b])
+                if b == 0:
+                    arrived(c, over)
+                z(c, b)
+                if b == last:
+                    for k in range(local):
+                        y(c, k)
+        for c in range(2):
+            for b in range(local):
+                arrived(c, fars[b])
+                z(c, local + b)
+                y(c, local + b)
+        arrived(0, *range(picks_inner, picks_inner + quota))
+        weigh(at)
+        arrived(1, *range(picks_inner, picks_inner + quota))
+        finish(at)
+        for c in range(2):
+            for n in range(2 * local):
+                sent(c, 2, n)
+            for n in range(1 + z_count):
+                sent(c, 0, n)
+            for n in range(1 + quota):
+                sent(c, 1, n)
+
+    @pl.when(at_end)
+    def _():
+        here, there = passed(mine + theirs)
+        sources = [*range(local), z_first, *range(z_rest, z_rest + z_count)]
+
+        def held(table, of_half):
+            names, slots_of = table
+            return [
+                *ids(end_view, of_half),
+                ids(inner_view, of_half)[0],
+                *(chosen(slots_of, names, k, jnp.int32(-2)) for k in range(z_count)),
+            ]
+
+        own_names, in_names = held(here, half), held(there, other)
+        y_slots = places([listed(theirs, name) for name in own_names], quota)
+        in_slots = places([listed(mine, name) for name in in_names], quota)
+        at = merge(
+            positions(own_names, [jnp.int32(j) for j in range(len(own_names))], 0),
+            positions(in_names, in_slots, picks_end),
+        )
+
+        def y(c, k):
+            stage(c, ystage, k, y_slots, sources, quota)
+            copy(c, 1, k, ystage.at[c, k], picks_end + k).start()
+
+        for part in range(2):
+            for c in range(2):
+                if part == 0:
+                    arrived(c, z_first)
+                for k in range(part * local, (part + 1) * local):
+                    arrived(c, z_rest + k)
+                    y(c, k)
+        arrived(0, *range(picks_end, picks_end + quota))
+        weigh(at)
+        arrived(1, *range(picks_end, picks_end + quota))
+        finish(at)
+        for c in range(2):
+            for n in range(local):
+                sent(c, 0, n)
+            for n in range(quota):
+                sent(c, 1, n)
+
+    for n, (to, device) in enumerate(list_routes):
+        for send in list_copies(to, device, n):
+            send.wait_send()
+
+
+def paired(sizes, block, tokens, w_qkv, lists, lens, inner):
+    rows, width = tokens.shape
+    local, slots = lists.shape
+    quota = local * slots
+    count = 4 * local + 1 + quota
+    anywhere = pl.BlockSpec(memory_space=pl.ANY)
+    return pl.pallas_call(
+        functools.partial(paired_body, sizes),
+        out_shape=pltpu.VMEM((rows, inner), jnp.bfloat16),
+        in_specs=[anywhere] * 4,
+        out_specs=pl.BlockSpec(memory_space=pltpu.VMEM),
+        scratch_shapes=[
+            pltpu.VMEM((rows, width), jnp.bfloat16),
+            pltpu.VMEM((3, width, inner), jnp.bfloat16),
+            pltpu.VMEM((count, block, inner), jnp.bfloat16),
+            pltpu.VMEM((count, block, inner), jnp.bfloat16),
+            pltpu.VMEM((2, quota, block, inner), jnp.bfloat16),
+            pltpu.VMEM((2, quota, block, inner), jnp.bfloat16),
+            pltpu.VMEM((local, HEADS * block, slots * block), jnp.bfloat16),
+            pltpu.VMEM((local, HEADS * block, 1), jnp.float32),
+            pltpu.SemaphoreType.DMA((local,)),
+            pltpu.SemaphoreType.DMA((3,)),
+            pltpu.SemaphoreType.DMA((2,)),
+            pltpu.SemaphoreType.DMA((2, 3, max(2 * local, 1 + quota))),
+            pltpu.SemaphoreType.DMA((2, count)),
+            pltpu.SemaphoreType.DMA((3, 2)),
+            pltpu.SemaphoreType.DMA((4, 2)),
+            *[pltpu.SMEM((local, slots), jnp.int32)] * 4,
+            *[pltpu.SMEM((local,), jnp.int32)] * 4,
+        ],
+        compiler_params=pltpu.CompilerParams(
+            collective_id=0, has_side_effects=True, vmem_limit_bytes=62000000
+        ),
+    )(lists, lens, tokens, w_qkv)
+
+
+def project_out(attn, w_out):
+    mixed = jnp.dot(attn, w_out, preferred_element_type=jnp.float32).astype(jnp.bfloat16)
+    return mixed.reshape(1, *mixed.shape)
+
+
 def per_device(sizes, tokens, w_qkv, w_out, key_lists, list_len):
     views, halves = sizes
     rows, width = tokens.shape[1:]
@@ -224,7 +623,18 @@
     slots = key_lists.shape[2]
     block = rows // local
     shards = views * halves
-    anywhere = pl.BlockSpec(memory_space=pltpu.HBM)
+    if views == 4 and halves == 2 and local == 2 and slots == 2:
+        attn = paired(
+            sizes,
+            block,
+            tokens.reshape(rows, width),
+            w_qkv,
+            key_lists.reshape(local, slots),
+            list_len.reshape(local),
+            inner,
+        )
+        return project_out(attn, w_out)
+    anywhere = pl.BlockSpec(memory_space=pl.ANY)
     attn = pl.pallas_call(
         functools.partial(body, sizes),
         out_shape=pltpu.VMEM((rows, inner), jnp.bfloat16),
@@ -257,8 +667,7 @@
         tokens.reshape(rows, width),
         w_qkv,
     )
-    mixed = jnp.dot(attn, w_out, preferred_element_type=jnp.float32).astype(jnp.bfloat16)
-    return mixed.reshape(1, rows, width)
+    return project_out(attn, w_out)
 
 
 def solution(mesh):

time: 29.6 us -> 27.5 us (0.929)
  Pallas kernels: 28 us -> 25.9 us
    pallas_call x1, Pallas kernels: 28 us -> 25.9 us  [paired(): pl.pallas_call(functools.partial(paired_body, sizes), out_shape=pltpu.VME...]
where the time goes in v2:
time: 27.5 us; the launch traced here: 27.4 us
  Pallas kernels  25.9 us (94%)
  matrix products  1.42 us (5%)
    pallas_call x1, Pallas kernels, paired(): pl.pallas_call(functools.partial(paired_body, sizes), out_shape=pltpu.VME...  25.9 us
    dot_general x1, matrix products, project_out(): jnp.dot(attn, w_out, preferred_element_type=jnp.float32)  1.42 us

profile of v2, /device:TPU:0, one launch (start us, length us, event | category | flops | bytes accessed | tf_op | source)
XLA Modules:
  0.0 27.4 jit_solution(15411317596568847768)
XLA Ops:
  0.0 0.0 copy-start
  0.0 25.9 %shard_map.55 = bf16[256,256]{1,0:T(8,128)(2,1)S(1)} custom-call(s32[2,2]{1,0:T(2,128)} %bitcast.8, s32[2]{0:T(128)} %bitcast.9, bf16[256,2048]{1,0:T(8,128)(2,1)} %bitcast.7, bf16[2048,768]{1,0:T(8,128)(2,1)} %w_ref.1), custom_call_target="tpu_custom_call" | custom-call | tf_op jit(solution)/shard_map/pallas_call | solution.py:583
  25.9 0.0 copy-done
  25.9 1.4 %fusion = bf16[1,256,2048]{2,1,0:T(8,128)(2,1)} fusion(bf16[256,256]{1,0:T(8,128)(2,1)S(1)} %shard_map.55, bf16[256,2048]{1,0:T(8,128)(2,1)S(1)} %copy-done), kind=kOutput, calls=%fused_computation.1 | convolution fusion | flops 268959744 | bytes 2228224 | tf_op jit(solution)/shard_map/dot_general | solution.py:614
Async XLA Ops:
  0.0 25.9 %copy-start = (bf16[256,2048]{1,0:T(8,128)(2,1)S(1)}, bf16[256,2048]{1,0:T(8,128)(2,1)}, u32[]{:S(2)}) copy-start(bf16[256,2048]{1,0:T(8,128)(2,1)} %param.7) | copy-start | bytes 3145732

commit v3 on v1

--- a/solution.py
+++ b/solution.py
@@ -216,6 +216,306 @@
             piece(c, slot, way).wait_send()
 
 
+def headwise_body(
+    sizes,
+    lists_hbm,
+    lens_hbm,
+    tokens_ref,
+    w_ref,
+    out_ref,
+    x,
+    w,
+    kbuf,
+    vbuf,
+    across,
+    queries,
+    results,
+    got,
+    weight_buf,
+    total_buf,
+    x_sem,
+    w_sem,
+    small_sem,
+    send_sem,
+    cross_sem,
+    recv_sem,
+    *small,
+):
+    views, halves = sizes
+    view, half = lax.axis_index("view"), lax.axis_index("half")
+    block, per = kbuf.shape[1:]
+    local = queries.shape[1]
+    inner = halves * per
+    head_size = inner // HEADS
+    shared = HEADS // halves
+    lists, lens = small[:4], small[4:]
+    slots = lists[0].shape[1]
+    bufs = (kbuf, vbuf)
+
+    loads = [
+        pltpu.make_async_copy(
+            tokens_ref.at[pl.ds(b * block, block)], x.at[pl.ds(b * block, block)], x_sem.at[b]
+        )
+        for b in range(local)
+    ]
+    w_loads = [
+        pltpu.make_async_copy(w_ref.at[:, pl.ds(group * inner, inner)], w.at[n], w_sem.at[n])
+        for n, group in enumerate((1, 2, 0))
+    ]
+    own_lists = [
+        pltpu.make_async_copy(lists_hbm, lists[0], small_sem.at[0]),
+        pltpu.make_async_copy(lens_hbm, lens[0], small_sem.at[1]),
+    ]
+    for load in (*loads, *w_loads, *own_lists):
+        load.start()
+
+    left = view < views // 2
+    end_view = jnp.where(left, 0, views - 1)
+    inner_view = jnp.where(left, 1, views - 2)
+    cross_view = views - 1 - inner_view
+    far_view = views - 1 - end_view
+    at_end = view == end_view
+    mate_view = jnp.where(at_end, inner_view, end_view)
+    other = halves - 1 - half
+    mate = {"view": mate_view}
+    beside = {"half": other}
+    diagonal = {"view": mate_view, "half": other}
+    cross = {"view": cross_view}
+
+    barrier = pltpu.get_barrier_semaphore()
+    for device in (mate, diagonal):
+        pl.semaphore_signal(barrier, inc=1, device_id=device, device_id_type=MESH)
+
+    @pl.when(jnp.logical_not(at_end))
+    def _():
+        for device in (beside, cross):
+            pl.semaphore_signal(barrier, inc=1, device_id=device, device_id_type=MESH)
+
+    def remote(src, dst, n, kind, device):
+        return pltpu.make_async_remote_copy(
+            src_ref=src,
+            dst_ref=dst,
+            send_sem=send_sem.at[n],
+            recv_sem=recv_sem.at[kind],
+            device_id=device,
+            device_id_type=MESH,
+        )
+
+    origins = (
+        (inner_view, other),
+        (end_view, half),
+        (end_view, other),
+        (cross_view, half),
+        (cross_view, other),
+        (far_view, half),
+        (far_view, other),
+    )
+    kinds = len(origins)
+    q_kind, r_kind, l_kind = 2 * kinds, 2 * kinds + 2, 2 * kinds + 4
+
+    def span(c, of_view, of_half):
+        return bufs[c].at[pl.ds((of_view * halves + of_half) * local, local)]
+
+    def onward(c, n):
+        rows = span(c, view, half) if n < 0 else span(c, *origins[n])
+        return pltpu.make_async_remote_copy(
+            src_ref=rows,
+            dst_ref=rows,
+            send_sem=cross_sem.at[c, n + 1],
+            recv_sem=recv_sem.at[c * kinds + n + 4],
+            device_id=cross,
+            device_id_type=MESH,
+        )
+
+    def arrived(c, n):
+        rows = span(c, *origins[n])
+        remote(rows, rows, 0, c * kinds + n, cross).wait_recv()
+
+    def to_row(c):
+        if c < 2:
+            return remote(span(c, view, half), span(c, view, half), c, c * kinds + 1, mate)
+        return remote(queries.at[0], queries.at[2], c, q_kind + 1, mate)
+
+    def to_other(c, device, origin):
+        if c < 2:
+            return remote(across.at[c], span(c, view, half), 3 + c, c * kinds + origin, device)
+        place = 1 if origin == 0 else 3
+        return remote(across.at[c], queries.at[place], 3 + c, q_kind + place - 1, device)
+
+    def list_copies(to, n, device):
+        return [
+            remote(src, dst, n + j, l_kind + 2 * (to - 1) + j, device)
+            for j, (src, dst) in enumerate(((lists_hbm, lists[to]), (lens_hbm, lens[to])))
+        ]
+
+    def place(c):
+        w_loads[c].wait()
+        for b in range(local):
+            if c == 0:
+                loads[b].wait()
+            y = jnp.dot(
+                x[b * block : (b + 1) * block], w[c], preferred_element_type=jnp.float32
+            ).astype(jnp.bfloat16)
+            own = jnp.where(half == 0, y[:, :per], y[:, per:])
+            across[c, b] = jnp.where(half == 0, y[:, per:], y[:, :per])
+            if c < 2:
+                bufs[c][(view * halves + half) * local + b] = own
+            else:
+                queries[0, b] = own
+
+    for c in range(3):
+        place(c)
+        if c == 0:
+            pl.semaphore_wait(barrier, jnp.where(at_end, 2, 4))
+
+        @pl.when(at_end)
+        def _():
+            to_row(c).start()
+            to_other(c, diagonal, 2).start()
+
+        @pl.when(jnp.logical_not(at_end))
+        def _():
+            if c < 2:
+                onward(c, -1).start()
+            to_other(c, beside, 0).start()
+
+    def assemble(own, rest):
+        for b in range(local):
+            rows = pl.ds(b * block, block)
+            out_ref[rows, :per] = jnp.where(half == 0, own[b], rest[b])
+            out_ref[rows, per:] = jnp.where(half == 0, rest[b], own[b])
+
+    head_of = lax.broadcasted_iota(jnp.int32, (block, per), 1) // head_size
+    heads = [head_of == h for h in range(shared)]
+
+    def weigh(g, i):
+        q = queries[g, i]
+        stacked = jnp.concatenate([jnp.where(m, q, jnp.zeros_like(q)) for m in heads], axis=0)
+        keys = jnp.concatenate([kbuf[lists[g][i, s]] for s in range(slots)], axis=0)
+        scores = lax.dot_general(
+            stacked, keys, (((1,), (1,)), ((), ())), preferred_element_type=jnp.float32
+        ) * head_size ** (-0.5)
+        live = lax.broadcasted_iota(jnp.int32, scores.shape, 1) // block < lens[g][i]
+        top = jnp.max(jnp.where(live, scores, NEG), axis=1, keepdims=True)
+        weights = jnp.where(live, jnp.exp(scores - top), 0.0)
+        total_buf[g * local + i] = jnp.sum(weights, axis=1, keepdims=True)
+        weight_buf[g * local + i] = weights.astype(jnp.bfloat16)
+
+    def finish(g, i):
+        values = jnp.concatenate([vbuf[lists[g][i, s]] for s in range(slots)], axis=0)
+        summed = jnp.dot(weight_buf[g * local + i], values, preferred_element_type=jnp.float32)
+        scaled = summed / total_buf[g * local + i]
+        attn = scaled[:block]
+        for h in range(1, shared):
+            attn = jnp.where(heads[h], scaled[h * block : (h + 1) * block], attn)
+        results[g, i] = attn.astype(jnp.bfloat16)
+
+    back = {
+        1: remote(results.at[1], got.at[1], 6, r_kind + 1, beside),
+        2: remote(results.at[2], got.at[0], 7, r_kind, mate),
+        3: remote(results.at[3], got.at[1], 8, r_kind + 1, diagonal),
+    }
+
+    for load in own_lists:
+        load.wait()
+
+    @pl.when(jnp.logical_not(at_end))
+    def _():
+        for send in list_copies(1, 9, beside):
+            send.start()
+        for c in range(2):
+            for n in range(3):
+                arrived(c, n)
+                onward(c, n).start()
+        for n in range(3):
+            remote(across.at[2], queries.at[n + 1], 0, q_kind + n, mate).wait_recv()
+        for to in (1, 2, 3):
+            for send in list_copies(to, 9, mate):
+                send.wait_recv()
+        for n in range(3, kinds):
+            arrived(0, n)
+        for g in (3, 2, 1, 0):
+            for i in range(local):
+                weigh(g, i)
+        for n in range(3, kinds):
+            arrived(1, n)
+        for g in (3, 2, 1, 0):
+            for i in range(local):
+                finish(g, i)
+            if g:
+                back[g].start()
+        back[1].wait_recv()
+        assemble(results.at[0], got.at[1])
+        for c in range(2):
+            for n in range(-1, 3):
+                onward(c, n).wait_send()
+        for c in range(3):
+            to_other(c, beside, 0).wait_send()
+        for g in (1, 2, 3):
+            back[g].wait_send()
+        for send in list_copies(1, 9, beside):
+            send.wait_send()
+
+    @pl.when(at_end)
+    def _():
+        routes = (list_copies(2, 9, mate), list_copies(3, 11, diagonal))
+        for route in routes:
+            for send in route:
+                send.start()
+        back[2].wait_recv()
+        back[3].wait_recv()
+        assemble(got.at[0], got.at[1])
+        for c in range(3):
+            to_row(c).wait_send()
+            to_other(c, diagonal, 2).wait_send()
+        for route in routes:
+            for send in route:
+                send.wait_send()
+
+
+def headwise(sizes, block, tokens, w_qkv, lists, lens, inner):
+    views, halves = sizes
+    rows, width = tokens.shape
+    local, slots = lists.shape
+    count, per = views * halves * local, inner // halves
+    stacked = HEADS // halves * block
+    anywhere = pl.BlockSpec(memory_space=pl.ANY)
+    return pl.pallas_call(
+        functools.partial(headwise_body, sizes),
+        out_shape=pltpu.VMEM((rows, inner), jnp.bfloat16),
+        in_specs=[anywhere] * 4,
+        out_specs=pl.BlockSpec(memory_space=pltpu.VMEM),
+        scratch_shapes=[
+            pltpu.VMEM((rows, width), jnp.bfloat16),
+            pltpu.VMEM((3, width, inner), jnp.bfloat16),
+            pltpu.VMEM((count, block, per), jnp.bfloat16),
+            pltpu.VMEM((count, block, per), jnp.bfloat16),
+            pltpu.VMEM((3, local, block, per), jnp.bfloat16),
+            pltpu.VMEM((4, local, block, per), jnp.bfloat16),
+            pltpu.VMEM((4, local, block, per), jnp.bfloat16),
+            pltpu.VMEM((2, local, block, per), jnp.bfloat16),
+            pltpu.VMEM((4 * local, stacked, slots * block), jnp.bfloat16),
+            pltpu.VMEM((4 * local, stacked, 1), jnp.float32),
+            pltpu.SemaphoreType.DMA((local,)),
+            pltpu.SemaphoreType.DMA((3,)),
+            pltpu.SemaphoreType.DMA((2,)),
+            pltpu.SemaphoreType.DMA((13,)),
+            pltpu.SemaphoreType.DMA((2, 4)),
+            pltpu.SemaphoreType.DMA((25,)),
+            *[pltpu.SMEM((local, slots), jnp.int32)] * 4,
+            *[pltpu.SMEM((local,), jnp.int32)] * 4,
+        ],
+        compiler_params=pltpu.CompilerParams(
+            collective_id=0, has_side_effects=True, vmem_limit_bytes=62000000
+        ),
+    )(lists, lens, tokens, w_qkv)
+
+
+def project_out(attn, w_out):
+    mixed = jnp.dot(attn, w_out, preferred_element_type=jnp.float32).astype(jnp.bfloat16)
+    return mixed.reshape(1, *mixed.shape)
+
+
 def per_device(sizes, tokens, w_qkv, w_out, key_lists, list_len):
     views, halves = sizes
     rows, width = tokens.shape[1:]
@@ -224,7 +524,18 @@
     slots = key_lists.shape[2]
     block = rows // local
     shards = views * halves
-    anywhere = pl.BlockSpec(memory_space=pltpu.HBM)
+    if views == 4 and halves == 2:
+        attn = headwise(
+            sizes,
+            block,
+            tokens.reshape(rows, width),
+            w_qkv,
+            key_lists.reshape(local, slots),
+            list_len.reshape(local),
+            inner,
+        )
+        return project_out(attn, w_out)
+    anywhere = pl.BlockSpec(memory_space=pl.ANY)
     attn = pl.pallas_call(
         functools.partial(body, sizes),
         out_shape=pltpu.VMEM((rows, inner), jnp.bfloat16),
@@ -257,8 +568,7 @@
         tokens.reshape(rows, width),
         w_qkv,
     )
-    mixed = jnp.dot(attn, w_out, preferred_element_type=jnp.float32).astype(jnp.bfloat16)
-    return mixed.reshape(1, rows, width)
+    return project_out(attn, w_out)
 
 
 def solution(mesh):

time: 29.6 us -> 25.2 us (0.85)
  Pallas kernels: 28 us -> 23.6 us
    pallas_call x1, Pallas kernels: 28 us -> 23.6 us  [headwise(): pl.pallas_call(functools.partial(headwise_body, sizes), out_shape=pltpu.V...]
where the time goes in v3:
time: 25.2 us; the launch traced here: 25 us
  Pallas kernels  23.6 us (94%)
  matrix products  1.42 us (6%)
    pallas_call x1, Pallas kernels, headwise(): pl.pallas_call(functools.partial(headwise_body, sizes), out_shape=pltpu.V...  23.6 us
    dot_general x1, matrix products, project_out(): jnp.dot(attn, w_out, preferred_element_type=jnp.float32)  1.42 us

profile of v3, /device:TPU:0, one launch (start us, length us, event | category | flops | bytes accessed | tf_op | source)
XLA Modules:
  0.0 25.0 jit_solution(6668453594350281813)
XLA Ops:
  0.0 0.0 copy-start
  0.0 23.6 %shard_map.55 = bf16[256,256]{1,0:T(8,128)(2,1)S(1)} custom-call(s32[2,2]{1,0:T(2,128)} %bitcast.8, s32[2]{0:T(128)} %bitcast.9, bf16[256,2048]{1,0:T(8,128)(2,1)} %bitcast.7, bf16[2048,768]{1,0:T(8,128)(2,1)} %w_ref.1), custom_call_target="tpu_custom_call" | custom-call | tf_op jit(solution)/shard_map/pallas_call | solution.py:483
  23.6 0.0 copy-done
  23.6 1.4 %fusion = bf16[1,256,2048]{2,1,0:T(8,128)(2,1)} fusion(bf16[256,256]{1,0:T(8,128)(2,1)S(1)} %shard_map.55, bf16[256,2048]{1,0:T(8,128)(2,1)S(1)} %copy-done), kind=kOutput, calls=%fused_computation.1 | convolution fusion | flops 268959744 | bytes 2228224 | tf_op jit(solution)/shard_map/dot_general | solution.py:515
Async XLA Ops:
  0.0 23.6 %copy-start = (bf16[256,2048]{1,0:T(8,128)(2,1)S(1)}, bf16[256,2048]{1,0:T(8,128)(2,1)}, u32[]{:S(2)}) copy-start(bf16[256,2048]{1,0:T(8,128)(2,1)} %param.7) | copy-start | bytes 3145732

commit v4 on v3

--- a/solution.py
+++ b/solution.py
@@ -9,6 +9,7 @@
 
 HEADS = 4
 NEG = -1e30
+STEPS = 4
 MESH = pl.DeviceIdType.MESH
 
 
@@ -242,6 +243,7 @@
     *small,
 ):
     views, halves = sizes
+    steps = x_sem.shape[0]
     view, half = lax.axis_index("view"), lax.axis_index("half")
     block, per = kbuf.shape[1:]
     local = queries.shape[1]
@@ -252,21 +254,28 @@
     slots = lists[0].shape[1]
     bufs = (kbuf, vbuf)
 
+    depth = x.shape[1] // steps
+    parts = [pl.ds(n * depth, depth) for n in range(steps)]
     loads = [
-        pltpu.make_async_copy(
-            tokens_ref.at[pl.ds(b * block, block)], x.at[pl.ds(b * block, block)], x_sem.at[b]
-        )
-        for b in range(local)
+        pltpu.make_async_copy(tokens_ref.at[:, part], x.at[:, part], x_sem.at[n])
+        for n, part in enumerate(parts)
+    ]
+    columns = [pl.ds(group * inner, inner) for group in (1, 2, 0)]
+    key_loads = [
+        pltpu.make_async_copy(w_ref.at[part, columns[0]], w.at[0, part], w_sem.at[2 + n])
+        for n, part in enumerate(parts)
     ]
     w_loads = [
-        pltpu.make_async_copy(w_ref.at[:, pl.ds(group * inner, inner)], w.at[n], w_sem.at[n])
-        for n, group in enumerate((1, 2, 0))
+        pltpu.make_async_copy(w_ref.at[:, columns[c]], w.at[c], w_sem.at[c - 1]) for c in (1, 2)
     ]
     own_lists = [
         pltpu.make_async_copy(lists_hbm, lists[0], small_sem.at[0]),
         pltpu.make_async_copy(lens_hbm, lens[0], small_sem.at[1]),
     ]
-    for load in (*loads, *w_loads, *own_lists):
+    for pair in zip(loads, key_loads):
+        for load in pair:
+            load.start()
+    for load in (*w_loads, *own_lists):
         load.start()
 
     left = view < views // 2
@@ -349,15 +358,20 @@
         ]
 
     def place(c):
-        w_loads[c].wait()
+        if c == 0:
+            y = jnp.zeros((local * block, inner), jnp.float32)
+            for n, part in enumerate(parts):
+                loads[n].wait()
+                key_loads[n].wait()
+                y += jnp.dot(x[:, part], w[c, part], preferred_element_type=jnp.float32)
+        else:
+            w_loads[c - 1].wait()
+            y = jnp.dot(x[...], w[c], preferred_element_type=jnp.float32)
+        y = y.astype(jnp.bfloat16)
         for b in range(local):
-            if c == 0:
-                loads[b].wait()
-            y = jnp.dot(
-                x[b * block : (b + 1) * block], w[c], preferred_element_type=jnp.float32
-            ).astype(jnp.bfloat16)
-            own = jnp.where(half == 0, y[:, :per], y[:, per:])
-            across[c, b] = jnp.where(half == 0, y[:, per:], y[:, :per])
+            rows = y[b * block : (b + 1) * block]
+            own = jnp.where(half == 0, rows[:, :per], rows[:, per:])
+            across[c, b] = jnp.where(half == 0, rows[:, per:], rows[:, :per])
             if c < 2:
                 bufs[c][(view * halves + half) * local + b] = own
             else:
@@ -375,9 +389,11 @@
 
         @pl.when(jnp.logical_not(at_end))
         def _():
-            if c < 2:
+            if c < 1:
                 onward(c, -1).start()
             to_other(c, beside, 0).start()
+            if c == 1:
+                onward(c, -1).start()
 
     def assemble(own, rest):
         for b in range(local):
@@ -423,10 +439,9 @@
     def _():
         for send in list_copies(1, 9, beside):
             send.start()
-        for c in range(2):
-            for n in range(3):
-                arrived(c, n)
-                onward(c, n).start()
+        for c, n in ((0, 0), (0, 1), (0, 2), (1, 0), (1, 1), (1, 2)):
+            arrived(c, n)
+            onward(c, n).start()
         for n in range(3):
             remote(across.at[2], queries.at[n + 1], 0, q_kind + n, mate).wait_recv()
         for to in (1, 2, 3):
@@ -439,7 +454,16 @@
                 weigh(g, i)
         for n in range(3, kinds):
             arrived(1, n)
-        for g in (3, 2, 1, 0):
+        for first, order in ((0, (2, 3)), (1, (3, 2))):
+
+            @pl.when(half == first)
+            def _():
+                for g in order:
+                    for i in range(local):
+                        finish(g, i)
+                    back[g].start()
+
+        for g in (1, 0):
             for i in range(local):
                 finish(g, i)
             if g:
@@ -496,8 +520,8 @@
             pltpu.VMEM((2, local, block, per), jnp.bfloat16),
             pltpu.VMEM((4 * local, stacked, slots * block), jnp.bfloat16),
             pltpu.VMEM((4 * local, stacked, 1), jnp.float32),
-            pltpu.SemaphoreType.DMA((local,)),
-            pltpu.SemaphoreType.DMA((3,)),
+            pltpu.SemaphoreType.DMA((STEPS,)),
+            pltpu.SemaphoreType.DMA((2 + STEPS,)),
             pltpu.SemaphoreType.DMA((2,)),
             pltpu.SemaphoreType.DMA((13,)),
             pltpu.SemaphoreType.DMA((2, 4)),
@@ -511,9 +535,32 @@
     )(lists, lens, tokens, w_qkv)
 
 
+def mix_body(attn_ref, w_ref, out_ref, buf, sem):
+    width = out_ref.shape[1]
+    step = width // 4
+    copies = []
+    for n in range(4):
+        cols = pl.ds(n * step, step)
+        buf[n] = jnp.dot(
+            attn_ref[...], w_ref[:, cols], preferred_element_type=jnp.float32
+        ).astype(jnp.bfloat16)
+        copies.append(pltpu.make_async_copy(buf.at[n], out_ref.at[:, cols], sem.at[n]))
+        copies[-1].start()
+    for copy in copies:
+        copy.wait()
+
+
 def project_out(attn, w_out):
-    mixed = jnp.dot(attn, w_out, preferred_element_type=jnp.float32).astype(jnp.bfloat16)
-    return mixed.reshape(1, *mixed.shape)
+    rows, width = attn.shape[0], w_out.shape[1]
+    mixed = pl.pallas_call(
+        mix_body,
+        out_shape=jax.ShapeDtypeStruct((rows, width), jnp.bfloat16),
+        in_specs=[pl.BlockSpec(memory_space=pltpu.VMEM), pl.BlockSpec(memory_space=pltpu.VMEM)],
+        out_specs=pl.BlockSpec(memory_space=pl.ANY),
+        scratch_shapes=[pltpu.VMEM((4, rows, width // 4), jnp.bfloat16), pltpu.SemaphoreType.DMA((4,))],
+        compiler_params=pltpu.CompilerParams(vmem_limit_bytes=16000000),
+    )(attn, w_out)
+    return mixed.reshape(1, rows, width)
 
 
 def per_device(sizes, tokens, w_qkv, w_out, key_lists, list_len):

time: 25.2 us -> 24.2 us (0.960)
  matrix products: 1.42 us -> 0 us
  Pallas kernels: 23.6 us -> 24.1 us
    dot_general x1 -> x0, matrix products: 1.42 us -> none  [project_out(): jnp.dot(attn, w_out, preferred_element_type=jnp.float32)]
    pallas_call x0 -> x1, Pallas kernels: none -> 1.23 us  [project_out(): pl.pallas_call(mix_body, out_shape=jax.ShapeDtypeStruct((rows, width), jn...]
    pallas_call x1, Pallas kernels: 23.6 us -> 22.8 us  [headwise(): pl.pallas_call(functools.partial(headwise_body, sizes), out_shape=pltpu.V...]
where the time goes in v4:
time: 24.2 us; the launch traced here: 24.1 us
  Pallas kernels  24.1 us (100%)
    pallas_call x1, Pallas kernels, headwise(): pl.pallas_call(functools.partial(headwise_body, sizes), out_shape=pltpu.V...  22.8 us
    pallas_call x1, Pallas kernels, project_out(): pl.pallas_call(mix_body, out_shape=jax.ShapeDtypeStruct((rows, width), jn...  1.23 us

profile of v4, /device:TPU:0, one launch (start us, length us, event | category | flops | bytes accessed | tf_op | source)
XLA Modules:
  0.0 24.1 jit_solution(10167375216779096190)
XLA Ops:
  0.0 0.0 copy-start
  0.0 22.8 %shard_map.55.attn_ref = bf16[256,256]{1,0:T(8,128)(2,1)S(1)} custom-call(s32[2,2]{1,0:T(2,128)} %bitcast.5, s32[2]{0:T(128)} %bitcast.6, bf16[256,2048]{1,0:T(8,128)(2,1)} %bitcast.4, bf16[2048,768]{1,0:T(8,128)(2,1)} %w_ref.2), custom_call_target="tpu_custom_call" | custom-call | tf_op jit(solution)/shard_map/pallas_call | solution.py:507
  22.8 0.0 copy-done
  22.9 1.2 %shard_map.56 = bf16[256,2048]{1,0:T(8,128)(2,1)} custom-call(bf16[256,256]{1,0:T(8,128)(2,1)S(1)} %shard_map.55.attn_ref, bf16[256,2048]{1,0:T(8,128)(2,1)S(1)} %copy-done), custom_call_target="tpu_custom_call" | custom-call | tf_op jit(solution)/shard_map/pallas_call | solution.py:555
Async XLA Ops:
  0.0 22.8 %copy-start = (bf16[256,2048]{1,0:T(8,128)(2,1)S(1)}, bf16[256,2048]{1,0:T(8,128)(2,1)}, u32[]{:S(2)}) copy-start(bf16[256,2048]{1,0:T(8,128)(2,1)} %w_ref.3) | copy-start | bytes 3145732

commit v5 on v4

--- a/solution.py
+++ b/solution.py
@@ -426,11 +426,10 @@
             attn = jnp.where(heads[h], scaled[h * block : (h + 1) * block], attn)
         results[g, i] = attn.astype(jnp.bfloat16)
 
-    back = {
-        1: remote(results.at[1], got.at[1], 6, r_kind + 1, beside),
-        2: remote(results.at[2], got.at[0], 7, r_kind, mate),
-        3: remote(results.at[3], got.at[1], 8, r_kind + 1, diagonal),
-    }
+    def returned(g, i):
+        place, device = ((1, beside), (0, mate), (1, diagonal))[g - 1]
+        kind = l_kind + 6 + place * local + i
+        return remote(results.at[g, i], got.at[place, i], 13 + (g - 1) * local + i, kind, device)
 
     for load in own_lists:
         load.wait()
@@ -461,14 +460,15 @@
                 for g in order:
                     for i in range(local):
                         finish(g, i)
-                    back[g].start()
+                        returned(g, i).start()
 
         for g in (1, 0):
             for i in range(local):
                 finish(g, i)
-            if g:
-                back[g].start()
-        back[1].wait_recv()
+                if g:
+                    returned(g, i).start()
+        for i in range(local):
+            returned(1, i).wait_recv()
         assemble(results.at[0], got.at[1])
         for c in range(2):
             for n in range(-1, 3):
@@ -476,7 +476,8 @@
         for c in range(3):
             to_other(c, beside, 0).wait_send()
         for g in (1, 2, 3):
-            back[g].wait_send()
+            for i in range(local):
+                returned(g, i).wait_send()
         for send in list_copies(1, 9, beside):
             send.wait_send()
 
@@ -486,8 +487,9 @@
         for route in routes:
             for send in route:
                 send.start()
-        back[2].wait_recv()
-        back[3].wait_recv()
+        for g in (2, 3):
+            for i in range(local):
+                returned(g, i).wait_recv()
         assemble(got.at[0], got.at[1])
         for c in range(3):
             to_row(c).wait_send()
@@ -523,9 +525,9 @@
             pltpu.SemaphoreType.DMA((STEPS,)),
             pltpu.SemaphoreType.DMA((2 + STEPS,)),
             pltpu.SemaphoreType.DMA((2,)),
-            pltpu.SemaphoreType.DMA((13,)),
+            pltpu.SemaphoreType.DMA((13 + 3 * local,)),
             pltpu.SemaphoreType.DMA((2, 4)),
-            pltpu.SemaphoreType.DMA((25,)),
+            pltpu.SemaphoreType.DMA((24 + 2 * local,)),
             *[pltpu.SMEM((local, slots), jnp.int32)] * 4,
             *[pltpu.SMEM((local,), jnp.int32)] * 4,
         ],

time: 24.2 us -> 24.3 us (level)
  no operation moved by 1% of the time
where the time goes in v5:
time: 24.3 us; the launch traced here: 24.1 us
  Pallas kernels  24.1 us (99%)
    pallas_call x1, Pallas kernels, headwise(): pl.pallas_call(functools.partial(headwise_body, sizes), out_shape=pltpu.V...  22.9 us
    pallas_call x1, Pallas kernels, project_out(): pl.pallas_call(mix_body, out_shape=jax.ShapeDtypeStruct((rows, width), jn...  1.23 us

profile of v5, /device:TPU:0, one launch (start us, length us, event | category | flops | bytes accessed | tf_op | source)
XLA Modules:
  0.0 24.1 jit_solution(12232500082733337707)
XLA Ops:
  0.0 0.0 copy-start
  0.0 22.9 %shard_map.55.attn_ref = bf16[256,256]{1,0:T(8,128)(2,1)S(1)} custom-call(s32[2,2]{1,0:T(2,128)} %bitcast.5, s32[2]{0:T(128)} %bitcast.6, bf16[256,2048]{1,0:T(8,128)(2,1)} %bitcast.4, bf16[2048,768]{1,0:T(8,128)(2,1)} %w_ref.2), custom_call_target="tpu_custom_call" | custom-call | tf_op jit(solution)/shard_map/pallas_call | solution.py:509
  22.9 0.0 copy-done
  22.9 1.2 %shard_map.56 = bf16[256,2048]{1,0:T(8,128)(2,1)} custom-call(bf16[256,256]{1,0:T(8,128)(2,1)S(1)} %shard_map.55.attn_ref, bf16[256,2048]{1,0:T(8,128)(2,1)S(1)} %copy-done), custom_call_target="tpu_custom_call" | custom-call | tf_op jit(solution)/shard_map/pallas_call | solution.py:557
Async XLA Ops:
  0.0 22.9 %copy-start = (bf16[256,2048]{1,0:T(8,128)(2,1)S(1)}, bf16[256,2048]{1,0:T(8,128)(2,1)}, u32[]{:S(2)}) copy-start(bf16[256,2048]{1,0:T(8,128)(2,1)} %w_ref.3) | copy-start | bytes 3145732
